TPU v7x, 256 devices: a whole 4x4x8 slice. The times are simulated.
256 devices in a mesh: dp: 32 (over z, y_lo, core), space: 8 (over x, y_hi).
Axes of the slice: x: 4, y: 4 (y_hi: 2, y_lo: 2; y = y_hi * 2 + y_lo), z: 8, core: 2. Of those that a mesh axis runs over, the one named last changes fastest.
Arguments:
- occupancy: int32 [32, 5, 128, 128], P('dp', None, 'space'), may hold values from 0 to 8191
- state_labels: int32 [32, 8, 8], P('dp', 'space'), may hold values 0 or 1
- lift_weight: bfloat16 [13, 32], replicated, may hold values from -1.75 to 1.75
- temporal_weight: bfloat16 [3, 3, 5, 32, 64], replicated, may hold values from -0.21875 to 0.21875
- middle_weight: bfloat16 [3, 3, 64, 128], replicated, may hold values from -0.375 to 0.375
- deeper_weight: bfloat16 [3, 3, 128, 256], replicated, may hold values from -0.25 to 0.25
- deepest_weight: bfloat16 [3, 3, 256, 512], replicated, may hold values from -0.1875 to 0.1875
- head_weight: bfloat16 [512], replicated, may hold values from -0.25 to 0.25
Outputs:
- temporal_grad: float32 [3, 3, 5, 32, 64], replicated
- middle_grad: float32 [3, 3, 64, 128], replicated
- deeper_grad: float32 [3, 3, 128, 256], replicated
- deepest_grad: float32 [3, 3, 256, 512], replicated
- head_grad: float32 [512], replicated
All inputs are finite; a program needn't handle non-finite values. No bound on the sum of `state_labels` on one device may be relied on, other than what follows from the above.
Results may differ from a plain program's by a relative error of at most 0.015.
Values may be sent and summed in bfloat16 or wider, within the bound.
A program may use at most 64 MiB of HBM per device.

v0:
```python
import jax
import jax.numpy as jnp
from jax import lax
from jax.sharding import PartitionSpec as P


def from_behind(block, axis, distance):
    devices = range(lax.axis_size(axis))
    route = [(i - distance, i) for i in devices if i - distance in devices]
    return lax.ppermute(block, axis, route)


def conv_layer(feature_map, weight):
    upper_row = from_behind(feature_map[:, :, -1:, :], "space", 1)
    padded = jnp.concatenate([upper_row, feature_map], axis=2)
    padded = jnp.pad(padded, ((0, 0), (0, 0), (0, 0), (1, 0)))
    accumulated = lax.conv_general_dilated(
        padded,
        weight,
        (2, 2),
        "VALID",
        dimension_numbers=("NCHW", "HWIO", "NCHW"),
        preferred_element_type=jnp.float32,
    )
    gate = jax.nn.sigmoid(accumulated)
    slope = gate * (1.0 + accumulated * (1.0 - gate))
    return ((accumulated * gate).astype(jnp.bfloat16), slope, padded)


def weight_grad(padded, delta):
    return lax.conv_general_dilated(
        padded,
        delta,
        (1, 1),
        "VALID",
        rhs_dilation=(2, 2),
        dimension_numbers=("CNHW", "IOHW", "HWNC"),
        preferred_element_type=jnp.float32,
    )


def input_grad(delta, weight):
    flipped = weight[::-1, ::-1]
    accumulated = lax.conv_general_dilated(
        delta,
        flipped,
        (1, 1),
        ((2, 2), (2, 2)),
        lhs_dilation=(2, 2),
        dimension_numbers=("NCHW", "HWOI", "NCHW"),
        preferred_element_type=jnp.float32,
    )
    lower_row = from_behind(accumulated[:, :, 0:1, 1:], "space", -1)
    local_part = accumulated[:, :, 1:, 1:]
    return jnp.concatenate([local_part[:, :, :-1], local_part[:, :, -1:] + lower_row], axis=2)


def local(
    occupancy,
    state_labels,
    lift_weight,
    temporal_weight,
    middle_weight,
    deeper_weight,
    deepest_weight,
    head_weight,
):
    samples_here = occupancy.shape[0]
    frames = occupancy.shape[1]
    heights = lift_weight.shape[0]
    lift_width = lift_weight.shape[1]
    shifts = jnp.arange(heights, dtype=jnp.int32)
    height_bits = jnp.bitwise_and(
        jnp.right_shift(occupancy[:, :, None], shifts[None, None, :, None, None]), 1
    ).astype(jnp.bfloat16)
    lifted = jnp.einsum(
        "stcrw,ck->stkrw", height_bits, lift_weight, preferred_element_type=jnp.float32
    )
    lifted = jnp.maximum(lifted, 0.0).astype(jnp.bfloat16)
    lifted = lifted.reshape(samples_here, frames * lift_width, lifted.shape[3], lifted.shape[4])
    first_kernel = temporal_weight.reshape(3, 3, frames * lift_width, temporal_weight.shape[4])
    first_map, first_slope, lifted_padded = conv_layer(lifted, first_kernel)
    second_map, second_slope, first_padded = conv_layer(first_map, middle_weight)
    third_map, third_slope, second_padded = conv_layer(second_map, deeper_weight)
    fourth_map, fourth_slope, third_padded = conv_layer(third_map, deepest_weight)
    batch_total = state_labels.shape[0] * lax.axis_size("dp")
    logits = jnp.einsum("sorw,o->srw", fourth_map, head_weight, preferred_element_type=jnp.float32)
    logit_grad = (jax.nn.sigmoid(logits) - state_labels.astype(jnp.float32)) / batch_total
    head_float = head_weight.astype(jnp.float32)
    head_grad = jnp.einsum("sorw,srw->o", fourth_map.astype(jnp.float32), logit_grad)
    fourth_delta = (logit_grad[:, None] * head_float[None, :, None, None] * fourth_slope).astype(
        jnp.bfloat16
    )
    deepest_grad = weight_grad(third_padded, fourth_delta)
    third_delta = (input_grad(fourth_delta, deepest_weight) * third_slope).astype(jnp.bfloat16)
    deeper_grad = weight_grad(second_padded, third_delta)
    second_delta = (input_grad(third_delta, deeper_weight) * second_slope).astype(jnp.bfloat16)
    middle_grad = weight_grad(first_padded, second_delta)
    first_delta = (input_grad(second_delta, middle_weight) * first_slope).astype(jnp.bfloat16)
    temporal_grad = weight_grad(lifted_padded, first_delta).reshape(temporal_weight.shape)
    reduced = lax.psum(
        (temporal_grad, middle_grad, deeper_grad, deepest_grad, head_grad), ("dp", "space")
    )
    return (reduced[0], reduced[1], reduced[2], reduced[3], reduced[4])


def solution(mesh):
    return jax.shard_map(
        local,
        mesh=mesh,
        in_specs=(
            P("dp", None, "space", None),
            P("dp", "space", None),
            P(),
            P(),
            P(),
            P(),
            P(),
            P(),
        ),
        out_specs=(P(), P(), P(), P(), P()),
        check_vma=False,
    )
```

profile of v0, /device:TPU:8, one launch (start us, length us, event | category | flops | bytes accessed | tf_op | source)
XLA Modules:
  0.0 403.2 jit_solution(4823248896462357719)
XLA Ops:
  7.2 1.3 fusion.9
  8.8 2.8 copy.146
  12.7 4.2 %collective-permute-start = (bf16[1,160,1,128]{1,0,3,2:T(2,128)(2,1)S(1)}, bf16[1,160,1,128]{1,0,3,2:T(2,128)(2,1)S(1)}, u32[]{:S(2)}, u32[]{:S(2)}) collective-permute-start(bf16[1,160,1,128]{1,0,3,2:T(2,128)(2,1)S(1)} %slice.81), channel_id=1, source_target_pairs={{0,1},{1,2},{2,3},{3,4},{4,5},{5,6},{6,7},{8,9},{9,10},{10,11},{11... | collective-permute-start | bytes 122888 | tf_op jit(solution)/shard_map/ppermute | solution.py:10
  16.9 2.7 collective-permute-done
  19.6 6.2 %pad_maximum_fusion = bf16[1,160,17,128]{1,0,3,2:T(2,128)(2,1)} fusion(bf16[1,160,16,128]{1,0,3,2:T(2,128)(2,1)} %copy.146, bf16[1,160,1,128]{1,0,3,2:T(2,128)(2,1)S(1)} %collective-permute-done), kind=kLoop, calls=%fused_computation.2 | loop fusion | flops 348160 | bytes 1392640 | tf_op jit(solution)/shard_map/concatenate | solution.py:15
  25.9 5.9 %copy.148 = bf16[1,160,17,128]{3,1,2,0:T(8,128)(2,1)} copy(bf16[1,160,17,128]{1,0,3,2:T(2,128)(2,1)} %pad_maximum_fusion) | data formatting | bytes 1392640 | tf_op jit(solution)/shard_map/concatenate | solution.py:15
  31.8 1.7 copy.200
  33.5 1.5 pad.8.clone
  35.0 3.4 reshape.106
  38.4 1.8 copy.151
  40.2 1.6 add_multiply_fusion
  41.9 5.9 %collective-permute-start.1 = (bf16[1,64,1,64]{1,0,3,2:T(2,128)(2,1)S(1)}, bf16[1,64,1,64]{1,0,3,2:T(2,128)(2,1)S(1)}, u32[]{:S(2)}, u32[]{:S(2)}) collective-permute-start(bf16[1,64,1,64]{1,0,3,2:T(2,128)(2,1)S(1)} %slice_bitcast_fusion.1), channel_id=1, source_target_pairs={{0,1},{1,2},{2,3},{3,4},{4,5},{5,6},{6,7},{8,9},{9,10},{10,11},{11... | collective-permute-start | bytes 24584 | tf_op jit(solution)/shard_map/ppermute | solution.py:10
  48.0 1.3 collective-permute-done.1
  50.4 1.9 add_multiply_fusion.1
  52.4 5.7 %collective-permute-start.2 = (bf16[1,128,1,32]{1,0,3,2:T(2,128)(2,1)S(1)}, bf16[1,128,1,32]{1,0,3,2:T(2,128)(2,1)S(1)}, u32[]{:S(2)}, u32[]{:S(2)}) collective-permute-start(bf16[1,128,1,32]{1,0,3,2:T(2,128)(2,1)S(1)} %slice_bitcast_fusion.3), channel_id=1, source_target_pairs={{0,1},{1,2},{2,3},{3,4},{4,5},{5,6},{6,7},{8,9},{9,10},{10,11},{11... | collective-permute-start | bytes 24584 | tf_op jit(solution)/shard_map/ppermute | solution.py:10
  58.2 1.3 collective-permute-done.2
  60.6 5.9 %collective-permute-start.3 = (bf16[1,256,1,16]{1,0,3,2:T(2,128)(2,1)S(1)}, bf16[1,256,1,16]{1,0,3,2:T(2,128)(2,1)S(1)}, u32[]{:S(2)}, u32[]{:S(2)}) collective-permute-start(bf16[1,256,1,16]{1,0,3,2:T(2,128)(2,1)S(1)} %slice_bitcast_fusion.2), channel_id=1, source_target_pairs={{0,1},{1,2},{2,3},{3,4},{4,5},{5,6},{6,7},{8,9},{9,10},{10,11},{11... | collective-permute-start | bytes 24584 | tf_op jit(solution)/shard_map/ppermute | solution.py:10
  70.7 1.5 collective-permute-start.4
  72.2 3.1 fusion.62
  75.2 3.8 collective-permute-done.4
  79.5 1.4 collective-permute-start.5
  80.9 1.5 fusion.85
  82.5 5.2 %collective-permute-done.5 = f32[1,128,1,32]{1,0,3,2:T(1,128)S(1)} collective-permute-done((f32[1,128,1,32]{1,0,3,2:T(1,128)S(1)}, f32[1,128,1,32]{1,0,3,2:T(1,128)S(1)}, u32[]{:S(2)}, u32[]{:S(2)}) %collective-permute-start.5) | collective-permute-done | bytes 16416 | tf_op jit(solution)/shard_map/ppermute | solution.py:10
  88.5 1.4 collective-permute-start.6
  89.9 2.5 fusion.93
  92.4 4.4 %collective-permute-done.6 = f32[1,64,1,64]{1,3,2,0:T(8,128)S(1)} collective-permute-done((f32[1,64,1,64]{1,3,2,0:T(8,128)S(1)}, f32[1,64,1,64]{1,3,2,0:T(8,128)S(1)}, u32[]{:S(2)}, u32[]{:S(2)}) %collective-permute-start.6) | collective-permute-done | bytes 16416 | tf_op jit(solution)/shard_map/ppermute | solution.py:10
  96.9 5.6 %fusion.25 = f32[3,3,160,64]{3,2,1,0:T(8,128)} fusion(bf16[1,160,17,128]{1,0,3,2:T(2,128)(2,1)S(1)} %copy-done.1, bf16[1,64,8,64]{1,3,2,0:T(8,128)(2,1)S(1)} %fusion.24), kind=kOutput, calls=%fused_computation.40 | convolution fusion | flops 93880320 | bytes 1130496 | tf_op jit(solution)/shard_map/conv_general_dilated | solution.py:31
  103.3 80.2 %psum.39 = f32[512]{0:T(512)} all-reduce(f32[512]{0:T(512)S(1)} %bitcast.187), channel_id=1, replica_groups=mesh['dp'=32,'space'=8] {'dp','space'}, use_global_device_ids=true, to_apply=%region_4.5 | all-reduce | flops 512 | bytes 4096 | tf_op jit(solution)/shard_map/psum | solution.py:101
  183.5 202.9 %all-reduce.3.cloned.1.call-done = (f32[3,3,5,32,64]{4,3,2,1,0:T(8,128)}, f32[3,3,64,128]{3,2,1,0:T(8,128)}, f32[3,3,128,256]{3,2,1,0:T(8,128)}, f32[3,3,256,512]{3,2,1,0:T(8,128)}) async-done(((f32[3,3,5,32,64]{4,3,2,1,0:T(8,128)}, f32[3,3,64,128]{3,2,1,0:T(8,128)}, f32[3,3,128,256]{3,2,1,0:T(8,128)}, f32[3,3,256,512]{3,2,1,0:T(8,128)}), (f32[3,3,5,32,64]{4,3,2,1,0:T(8,128)}, f32[3,3,64,128]{3,2,1,0:T(8,128)}, ...) | async-done | bytes 6561808 | tf_op jit(solution)/shard_map/psum | solution.py:101
  386.4 2.1 copy.241
  388.6 1.7 copy.242
  391.3 5.0 %copy.244 = f32[3,3,256,512]{3,2,1,0:T(8,128)} copy(f32[3,3,256,512]{3,2,1,0:T(8,128)} %get-tuple-element.22) | data formatting | bytes 9437184
  (125 shorter events, 10.8 us)
Async XLA Ops:
  7.2 61.5 %copy-start = (bf16[3,3,256,512]{3,2,1,0:T(8,128)(2,1)S(1)}, bf16[3,3,256,512]{3,2,1,0:T(8,128)(2,1)}, u32[]{:S(2)}) copy-start(bf16[3,3,256,512]{3,2,1,0:T(8,128)(2,1)} %param.14) | copy-start | bytes 7077892
  7.2 379.3 %all-reduce.3.cloned.1.call-start = ((), (), s32[]{:S(2)}) async-start(), calls=%async_computation | async-start | bytes 13860864 | tf_op jit(solution)/shard_map/psum | solution.py:101
  12.7 6.9 %collective-permute-start = (bf16[1,160,1,128]{1,0,3,2:T(2,128)(2,1)S(1)}, bf16[1,160,1,128]{1,0,3,2:T(2,128)(2,1)S(1)}, u32[]{:S(2)}, u32[]{:S(2)}) collective-permute-start(bf16[1,160,1,128]{1,0,3,2:T(2,128)(2,1)S(1)} %slice.81), channel_id=1, source_target_pairs={{0,1},{1,2},{2,3},{3,4},{4,5},{5,6},{6,7},{8,9},{9,10},{10,11},{11... | collective-permute-start | bytes 122888 | tf_op jit(solution)/shard_map/ppermute | solution.py:10
  38.3 1.8 copy-start.15
  38.3 1.8 copy-start.17
  41.8 8.6 %copy-start.18 = (pred[8,5]{0,1:T(8,128)(4,1)S(1)}, pred[8,5]{0,1:T(8,128)(4,1)}, u32[]{:S(2)}) copy-start(pred[8,5]{0,1:T(8,128)(4,1)} %constant.40) | copy-start | bytes 124
  41.9 7.5 %collective-permute-start.1 = (bf16[1,64,1,64]{1,0,3,2:T(2,128)(2,1)S(1)}, bf16[1,64,1,64]{1,0,3,2:T(2,128)(2,1)S(1)}, u32[]{:S(2)}, u32[]{:S(2)}) collective-permute-start(bf16[1,64,1,64]{1,0,3,2:T(2,128)(2,1)S(1)} %slice_bitcast_fusion.1), channel_id=1, source_target_pairs={{0,1},{1,2},{2,3},{3,4},{4,5},{5,6},{6,7},{8,9},{9,10},{10,11},{11... | collective-permute-start | bytes 24584 | tf_op jit(solution)/shard_map/ppermute | solution.py:10
  49.8 10.7 %copy-start.3 = (bf16[1,64,9,64]{1,0,3,2:T(2,128)(2,1)}, bf16[1,64,9,64]{1,0,3,2:T(2,128)(2,1)S(1)}, u32[]{:S(2)}) copy-start(bf16[1,64,9,64]{1,0,3,2:T(2,128)(2,1)S(1)} %pad_maximum_fusion.1) | copy-start | bytes 221188
  49.8 10.4 %copy-start.19 = (pred[8,3]{0,1:T(4,128)(4,1)S(1)}, pred[8,3]{0,1:T(4,128)(4,1)}, u32[]{:S(2)}) copy-start(pred[8,3]{0,1:T(4,128)(4,1)} %constant.39) | copy-start | bytes 76
  50.2 16.3 %copy-start.10 = (bf16[512]{0:T(512)(128)(2,1)S(1)}, bf16[512]{0:T(512)(128)(2,1)}, u32[]{:S(2)}) copy-start(bf16[512]{0:T(512)(128)(2,1)} %param.15) | copy-start | bytes 3076
  50.3 9.9 %copy-start.5 = (bf16[3,3,128,256]{3,2,1,0:T(8,128)(2,1)S(1)}, bf16[3,3,128,256]{3,2,1,0:T(8,128)(2,1)}, u32[]{:S(2)}) copy-start(bf16[3,3,128,256]{3,2,1,0:T(8,128)(2,1)} %param.13) | copy-start | bytes 1769476
  52.3 16.3 %copy-start.14 = (pred[8,2]{0,1:T(4,128)(4,1)S(1)}, pred[8,2]{0,1:T(4,128)(4,1)}, u32[]{:S(2)}) copy-start(pred[8,2]{0,1:T(4,128)(4,1)} %constant.38) | copy-start | bytes 52
  52.4 7.2 %collective-permute-start.2 = (bf16[1,128,1,32]{1,0,3,2:T(2,128)(2,1)S(1)}, bf16[1,128,1,32]{1,0,3,2:T(2,128)(2,1)S(1)}, u32[]{:S(2)}, u32[]{:S(2)}) collective-permute-start(bf16[1,128,1,32]{1,0,3,2:T(2,128)(2,1)S(1)} %slice_bitcast_fusion.3), channel_id=1, source_target_pairs={{0,1},{1,2},{2,3},{3,4},{4,5},{5,6},{6,7},{8,9},{9,10},{10,11},{11... | collective-permute-start | bytes 24584 | tf_op jit(solution)/shard_map/ppermute | solution.py:10
  59.5 0.6 copy-start.8
  60.1 8.1 %copy-start.7 = (f32[4,8,5,128]{3,1,2,0:T(8,128)S(1)}, f32[4,8,5,128]{3,1,2,0:T(8,128)}, u32[]{:S(2)}) copy-start(f32[4,8,5,128]{3,1,2,0:T(8,128)} %get-tuple-element.11) | copy-start | bytes 245764
  60.6 7.9 %collective-permute-start.3 = (bf16[1,256,1,16]{1,0,3,2:T(2,128)(2,1)S(1)}, bf16[1,256,1,16]{1,0,3,2:T(2,128)(2,1)S(1)}, u32[]{:S(2)}, u32[]{:S(2)}) collective-permute-start(bf16[1,256,1,16]{1,0,3,2:T(2,128)(2,1)S(1)} %slice_bitcast_fusion.2), channel_id=1, source_target_pairs={{0,1},{1,2},{2,3},{3,4},{4,5},{5,6},{6,7},{8,9},{9,10},{10,11},{11... | collective-permute-start | bytes 24584 | tf_op jit(solution)/shard_map/ppermute | solution.py:10
  67.5 1.7 copy-start.16
  69.3 0.5 copy-start.12
  70.7 10.3 %copy-start.9 = (bf16[1,128,1,32]{1,0,3,2:T(2,128)(2,1)S(1)}, bf16[1,128,1,32]{1,0,3,2:T(2,128)(2,1)}, u32[]{:S(2)}) copy-start(bf16[1,128,1,32]{1,0,3,2:T(2,128)(2,1)} %copy-done.8) | copy-start | bytes 24580
  70.7 8.3 %collective-permute-start.4 = (f32[1,256,1,16]{1,0,3,2:T(1,128)S(1)}, f32[1,256,1,16]{1,0,3,2:T(1,128)S(1)}, u32[]{:S(2)}, u32[]{:S(2)}) collective-permute-start(f32[1,256,1,16]{1,0,3,2:T(1,128)S(1)} %get-tuple-element.14), channel_id=1, source_target_pairs={{1,0},{2,1},{3,2},{4,3},{5,4},{6,5},{7,6},{9,8},{10,9},{11,10},{12... | collective-permute-start | bytes 49160 | tf_op jit(solution)/shard_map/ppermute | solution.py:10
  79.5 8.4 %copy-start.6 = (bf16[3,3,64,128]{3,2,1,0:T(8,128)(2,1)S(1)}, bf16[3,3,64,128]{3,2,1,0:T(8,128)(2,1)}, u32[]{:S(2)}) copy-start(bf16[3,3,64,128]{3,2,1,0:T(8,128)(2,1)} %param.12) | copy-start | bytes 442372
  79.5 8.4 %copy-start.11 = (pred[8,10]{0,1:T(8,128)(4,1)S(1)}, pred[8,10]{0,1:T(8,128)(4,1)}, u32[]{:S(2)}) copy-start(pred[8,10]{0,1:T(8,128)(4,1)} %constant.37) | copy-start | bytes 244
  79.5 8.2 %collective-permute-start.5 = (f32[1,128,1,32]{1,0,3,2:T(1,128)S(1)}, f32[1,128,1,32]{1,0,3,2:T(1,128)S(1)}, u32[]{:S(2)}, u32[]{:S(2)}) collective-permute-start(f32[1,128,1,32]{1,0,3,2:T(1,128)S(1)} %slice.103), channel_id=1, source_target_pairs={{1,0},{2,1},{3,2},{4,3},{5,4},{6,5},{7,6},{9,8},{10,9},{11,10},{12... | collective-permute-start | bytes 49160 | tf_op jit(solution)/shard_map/ppermute | solution.py:10
  88.5 8.4 %copy-start.4 = (f32[8,1,64,64]{3,0,2,1:T(8,128)S(1)}, f32[8,1,64,64]{3,0,2,1:T(8,128)}, u32[]{:S(2)}) copy-start(f32[8,1,64,64]{3,0,2,1:T(8,128)} %slice.110) | copy-start | bytes 393220
  88.5 8.4 %copy-start.1 = (bf16[1,160,17,128]{1,0,3,2:T(2,128)(2,1)S(1)}, bf16[1,160,17,128]{1,0,3,2:T(2,128)(2,1)}, u32[]{:S(2)}) copy-start(bf16[1,160,17,128]{1,0,3,2:T(2,128)(2,1)} %pad_maximum_fusion) | copy-start | bytes 2088964
  88.5 8.3 %collective-permute-start.6 = (f32[1,64,1,64]{1,3,2,0:T(8,128)S(1)}, f32[1,64,1,64]{1,3,2,0:T(8,128)S(1)}, u32[]{:S(2)}, u32[]{:S(2)}) collective-permute-start(f32[1,64,1,64]{1,3,2,0:T(8,128)S(1)} %slice.109), channel_id=1, source_target_pairs={{1,0},{2,1},{3,2},{4,3},{5,4},{6,5},{7,6},{9,8},{10,9},{11,10},{12... | collective-permute-start | bytes 49160 | tf_op jit(solution)/shard_map/ppermute | solution.py:10
  102.5 0.7 copy-start.13
  386.4 3.8 copy-start.2
Sparse Core Ops, SparseCore 0:
  102.7 283.7 all-reduce.2
where the time goes:
time: 404 us; the launch traced here: 403 us
  waiting for transfers between devices  222 us (55%)
  blocking collectives  80.2 us (20%)
  local copies, waits for them, and re-layouts  33.2 us (8%)
  starting transfers between devices  26 us (6%)
  matrix products  20 us (5%)
  between operations  14.8 us (4%)
  other arithmetic  7.19 us (2%)
    psum x1, waiting for transfers between devices, local(): lax.psum((temporal_grad, middle_grad, deeper_grad, deepest_grad, head_gra...  203 us
    psum x1, blocking collectives, local(): lax.psum((temporal_grad, middle_grad, deeper_grad, deepest_grad, head_gra...  80.2 us
    ppermute x7, starting transfers between devices, from_behind(): return lax.ppermute(block, axis, route)  26 us
    ppermute x7, waiting for transfers between devices, from_behind(): return lax.ppermute(block, axis, route)  18.8 us
    unnamed x54, local copies, waits for them, and re-layouts  13.6 us
    conv_general_dilated x4, matrix products, weight_grad(): lax.conv_general_dilated(padded, delta, (1, 1), 'VALID', rhs_dilation=(2,...  12.7 us
  transfers between devices with their start and end apart: 8, of which 7 were waited for; matrix products, arithmetic and copies ran while one was open for 2% of the time, Pallas kernels for 0%

commit v1 on v0

--- a/solution.py
+++ b/solution.py
@@ -2,6 +2,7 @@
 import jax.numpy as jnp
 from jax import lax
 from jax.sharding import PartitionSpec as P
+from jax.lax import psum
 
 
 def from_behind(block, axis, distance):
@@ -98,9 +99,9 @@
     middle_grad = weight_grad(first_padded, second_delta)
     first_delta = (input_grad(second_delta, middle_weight) * first_slope).astype(jnp.bfloat16)
     temporal_grad = weight_grad(lifted_padded, first_delta).reshape(temporal_weight.shape)
-    reduced = lax.psum(
-        (temporal_grad, middle_grad, deeper_grad, deepest_grad, head_grad), ("dp", "space")
-    )
+    reduced = (temporal_grad, middle_grad, deeper_grad, deepest_grad, head_grad)
+    for dev in ("dp", "space"):
+        reduced = psum(reduced, dev)
     return (reduced[0], reduced[1], reduced[2], reduced[3], reduced[4])
 
 

time: 404 us -> 677 us (1.68)
  waiting for transfers between devices: 222 us -> 463 us
  blocking collectives: 80.2 us -> 106 us
    psum x1 -> x2, waiting for transfers between devices: 203 us -> 444 us  [local(): reduced = psum(reduced, dev)]
    psum x1 -> x2, blocking collectives: 80.2 us -> 106 us  [local(): reduced = psum(reduced, dev)]
  transfers between devices with their start and end apart: 8 -> 9, of which waited for: 7 -> 8; matrix products, arithmetic and copies ran while one was open for 2% -> 1% of each run, Pallas kernels for 0% -> 0%
where the time goes in v1:
time: 677 us; the launch traced here: 670 us
  waiting for transfers between devices  463 us (68%)
  blocking collectives  106 us (16%)
  local copies, waits for them, and re-layouts  33.2 us (5%)
  starting transfers between devices  26.1 us (4%)
  matrix products  20 us (3%)
  between operations  14.8 us (2%)
  other arithmetic  7.2 us (1%)
    psum x2, waiting for transfers between devices, local(): reduced = psum(reduced, dev)  444 us
    psum x2, blocking collectives, local(): reduced = psum(reduced, dev)  106 us
    ppermute x7, starting transfers between devices, from_behind(): return lax.ppermute(block, axis, route)  26 us
    ppermute x7, waiting for transfers between devices, from_behind(): return lax.ppermute(block, axis, route)  18.8 us
    unnamed x54, local copies, waits for them, and re-layouts  13.6 us
  transfers between devices with their start and end apart: 9, of which 8 were waited for; matrix products, arithmetic and copies ran while one was open for 1% of the time, Pallas kernels for 0%

profile of v1, /device:TPU:8, one launch (start us, length us, event | category | flops | bytes accessed | tf_op | source)
XLA Modules:
  0.0 669.8 jit_solution(14238176099312989811)
XLA Ops:
  8.8 2.8 copy.146
  12.7 4.2 collective-permute-start
  16.9 2.7 collective-permute-done
  19.6 6.2 pad_maximum_fusion
  25.9 5.9 copy.148
  31.8 1.7 copy.200
  33.5 1.5 pad.8.clone
  35.0 3.4 reshape.106
  38.4 1.8 copy.151
  40.2 1.6 add_multiply_fusion
  41.9 5.9 collective-permute-start.1
  48.0 1.3 collective-permute-done.1
  50.4 1.9 add_multiply_fusion.1
  52.4 5.7 collective-permute-start.2
  60.6 5.9 collective-permute-start.3
  70.7 1.5 collective-permute-start.4
  72.2 3.1 fusion.62
  75.2 3.8 collective-permute-done.4
  79.5 1.4 collective-permute-start.5
  80.9 1.5 fusion.85
  82.5 5.2 collective-permute-done.5
  88.5 1.4 collective-permute-start.6
  89.9 2.5 fusion.93
  92.4 4.4 collective-permute-done.6
  96.9 5.6 fusion.25
  102.6 250.5 %all-reduce.5.cloned.1.call-done = (f32[3,3,5,32,64]{4,3,2,1,0:T(8,128)}, f32[3,3,64,128]{3,2,1,0:T(8,128)}, f32[3,3,128,256]{3,2,1,0:T(8,128)}, f32[3,3,256,512]{3,2,1,0:T(8,128)}) async-done(((f32[3,3,5,32,64]{4,3,2,1,0:T(8,128)}, f32[3,3,64,128]{3,2,1,0:T(8,128)}, f32[3,3,128,256]{3,2,1,0:T(8,128)}, f32[3,3,256,512]{3,2,1,0:T(8,128)}), (f32[3,3,5,32,64]{4,3,2,1,0:T(8,128)}, f32[3,3,64,128]{3,2,1,0:T(8,128)}, ...) | async-done | bytes 6561808 | tf_op jit(solution)/shard_map/psum | solution.py:104
  353.9 67.0 %psum.78 = f32[512]{0:T(512)S(1)} all-reduce(f32[512]{0:T(512)S(1)} %bitcast.187), channel_id=1, replica_groups=mesh['dp'=32,'space'=8] {'dp'}, use_global_device_ids=true, to_apply=%region_8.9 | all-reduce | flops 512 | bytes 4096 | tf_op jit(solution)/shard_map/psum | solution.py:104
  421.0 38.5 %psum.79 = f32[512]{0:T(512)} all-reduce(f32[512]{0:T(512)S(1)} %psum.78), channel_id=1, replica_groups=mesh['dp'=32,'space'=8] {'space'}, use_global_device_ids=true, to_apply=%region_9.10 | all-reduce | flops 512 | bytes 4096 | tf_op jit(solution)/shard_map/psum | solution.py:104
  459.5 193.6 %all-reduce.7.cloned.1.call-done = (f32[3,3,5,32,64]{4,3,2,1,0:T(8,128)}, f32[3,3,64,128]{3,2,1,0:T(8,128)}, f32[3,3,128,256]{3,2,1,0:T(8,128)}, f32[3,3,256,512]{3,2,1,0:T(8,128)}) async-done(((f32[3,3,5,32,64]{4,3,2,1,0:T(8,128)}, f32[3,3,64,128]{3,2,1,0:T(8,128)}, f32[3,3,128,256]{3,2,1,0:T(8,128)}, f32[3,3,256,512]{3,2,1,0:T(8,128)}), (f32[3,3,5,32,64]{4,3,2,1,0:T(8,128)}, f32[3,3,64,128]{3,2,1,0:T(8,128)}, ...) | async-done | bytes 6561808 | tf_op jit(solution)/shard_map/psum | solution.py:104
  653.1 2.1 copy.245
  655.2 1.7 copy.246
  657.9 5.0 copy.248
  (129 shorter events, 13.5 us)
Async XLA Ops:
  7.2 61.5 %copy-start = (bf16[3,3,256,512]{3,2,1,0:T(8,128)(2,1)S(1)}, bf16[3,3,256,512]{3,2,1,0:T(8,128)(2,1)}, u32[]{:S(2)}) copy-start(bf16[3,3,256,512]{3,2,1,0:T(8,128)(2,1)} %param.14) | copy-start | bytes 7077892
  7.2 346.0 %all-reduce.5.cloned.1.call-start = ((), (), s32[]{:S(2)}) async-start(), calls=%async_computation | async-start | bytes 13860864 | tf_op jit(solution)/shard_map/psum | solution.py:104
  12.7 6.9 %collective-permute-start = (bf16[1,160,1,128]{1,0,3,2:T(2,128)(2,1)S(1)}, bf16[1,160,1,128]{1,0,3,2:T(2,128)(2,1)S(1)}, u32[]{:S(2)}, u32[]{:S(2)}) collective-permute-start(bf16[1,160,1,128]{1,0,3,2:T(2,128)(2,1)S(1)} %slice.81), channel_id=1, source_target_pairs={{0,1},{1,2},{2,3},{3,4},{4,5},{5,6},{6,7},{8,9},{9,10},{10,11},{11... | collective-permute-start | bytes 122888 | tf_op jit(solution)/shard_map/ppermute | solution.py:11
  38.4 1.8 copy-start.15
  38.4 1.8 copy-start.17
  41.8 8.6 %copy-start.18 = (pred[8,5]{0,1:T(8,128)(4,1)S(1)}, pred[8,5]{0,1:T(8,128)(4,1)}, u32[]{:S(2)}) copy-start(pred[8,5]{0,1:T(8,128)(4,1)} %constant.40) | copy-start | bytes 124
  41.9 7.5 %collective-permute-start.1 = (bf16[1,64,1,64]{1,0,3,2:T(2,128)(2,1)S(1)}, bf16[1,64,1,64]{1,0,3,2:T(2,128)(2,1)S(1)}, u32[]{:S(2)}, u32[]{:S(2)}) collective-permute-start(bf16[1,64,1,64]{1,0,3,2:T(2,128)(2,1)S(1)} %slice_bitcast_fusion.1), channel_id=1, source_target_pairs={{0,1},{1,2},{2,3},{3,4},{4,5},{5,6},{6,7},{8,9},{9,10},{10,11},{11... | collective-permute-start | bytes 24584 | tf_op jit(solution)/shard_map/ppermute | solution.py:11
  49.8 10.7 %copy-start.3 = (bf16[1,64,9,64]{1,0,3,2:T(2,128)(2,1)}, bf16[1,64,9,64]{1,0,3,2:T(2,128)(2,1)S(1)}, u32[]{:S(2)}) copy-start(bf16[1,64,9,64]{1,0,3,2:T(2,128)(2,1)S(1)} %pad_maximum_fusion.1) | copy-start | bytes 221188
  49.8 10.4 %copy-start.19 = (pred[8,3]{0,1:T(4,128)(4,1)S(1)}, pred[8,3]{0,1:T(4,128)(4,1)}, u32[]{:S(2)}) copy-start(pred[8,3]{0,1:T(4,128)(4,1)} %constant.39) | copy-start | bytes 76
  50.2 16.3 %copy-start.10 = (bf16[512]{0:T(512)(128)(2,1)S(1)}, bf16[512]{0:T(512)(128)(2,1)}, u32[]{:S(2)}) copy-start(bf16[512]{0:T(512)(128)(2,1)} %param.15) | copy-start | bytes 3076
  50.3 9.9 %copy-start.5 = (bf16[3,3,128,256]{3,2,1,0:T(8,128)(2,1)S(1)}, bf16[3,3,128,256]{3,2,1,0:T(8,128)(2,1)}, u32[]{:S(2)}) copy-start(bf16[3,3,128,256]{3,2,1,0:T(8,128)(2,1)} %param.13) | copy-start | bytes 1769476
  52.3 16.3 %copy-start.14 = (pred[8,2]{0,1:T(4,128)(4,1)S(1)}, pred[8,2]{0,1:T(4,128)(4,1)}, u32[]{:S(2)}) copy-start(pred[8,2]{0,1:T(4,128)(4,1)} %constant.38) | copy-start | bytes 52
  52.4 7.2 %collective-permute-start.2 = (bf16[1,128,1,32]{1,0,3,2:T(2,128)(2,1)S(1)}, bf16[1,128,1,32]{1,0,3,2:T(2,128)(2,1)S(1)}, u32[]{:S(2)}, u32[]{:S(2)}) collective-permute-start(bf16[1,128,1,32]{1,0,3,2:T(2,128)(2,1)S(1)} %slice_bitcast_fusion.3), channel_id=1, source_target_pairs={{0,1},{1,2},{2,3},{3,4},{4,5},{5,6},{6,7},{8,9},{9,10},{10,11},{11... | collective-permute-start | bytes 24584 | tf_op jit(solution)/shard_map/ppermute | solution.py:11
  59.5 0.6 copy-start.8
  60.2 8.1 %copy-start.7 = (f32[4,8,5,128]{3,1,2,0:T(8,128)S(1)}, f32[4,8,5,128]{3,1,2,0:T(8,128)}, u32[]{:S(2)}) copy-start(f32[4,8,5,128]{3,1,2,0:T(8,128)} %get-tuple-element.15) | copy-start | bytes 245764
  60.6 7.9 %collective-permute-start.3 = (bf16[1,256,1,16]{1,0,3,2:T(2,128)(2,1)S(1)}, bf16[1,256,1,16]{1,0,3,2:T(2,128)(2,1)S(1)}, u32[]{:S(2)}, u32[]{:S(2)}) collective-permute-start(bf16[1,256,1,16]{1,0,3,2:T(2,128)(2,1)S(1)} %slice_bitcast_fusion.2), channel_id=1, source_target_pairs={{0,1},{1,2},{2,3},{3,4},{4,5},{5,6},{6,7},{8,9},{9,10},{10,11},{11... | collective-permute-start | bytes 24584 | tf_op jit(solution)/shard_map/ppermute | solution.py:11
  67.5 1.6 copy-start.16
  69.3 0.5 copy-start.12
  70.7 10.3 %copy-start.9 = (bf16[1,128,1,32]{1,0,3,2:T(2,128)(2,1)S(1)}, bf16[1,128,1,32]{1,0,3,2:T(2,128)(2,1)}, u32[]{:S(2)}) copy-start(bf16[1,128,1,32]{1,0,3,2:T(2,128)(2,1)} %copy-done.8) | copy-start | bytes 24580
  70.7 8.3 %collective-permute-start.4 = (f32[1,256,1,16]{1,0,3,2:T(1,128)S(1)}, f32[1,256,1,16]{1,0,3,2:T(1,128)S(1)}, u32[]{:S(2)}, u32[]{:S(2)}) collective-permute-start(f32[1,256,1,16]{1,0,3,2:T(1,128)S(1)} %get-tuple-element.18), channel_id=1, source_target_pairs={{1,0},{2,1},{3,2},{4,3},{5,4},{6,5},{7,6},{9,8},{10,9},{11,10},{12... | collective-permute-start | bytes 49160 | tf_op jit(solution)/shard_map/ppermute | solution.py:11
  79.5 8.4 %copy-start.6 = (bf16[3,3,64,128]{3,2,1,0:T(8,128)(2,1)S(1)}, bf16[3,3,64,128]{3,2,1,0:T(8,128)(2,1)}, u32[]{:S(2)}) copy-start(bf16[3,3,64,128]{3,2,1,0:T(8,128)(2,1)} %param.12) | copy-start | bytes 442372
  79.5 8.4 %copy-start.11 = (pred[8,10]{0,1:T(8,128)(4,1)S(1)}, pred[8,10]{0,1:T(8,128)(4,1)}, u32[]{:S(2)}) copy-start(pred[8,10]{0,1:T(8,128)(4,1)} %constant.37) | copy-start | bytes 244
  79.5 8.2 %collective-permute-start.5 = (f32[1,128,1,32]{1,0,3,2:T(1,128)S(1)}, f32[1,128,1,32]{1,0,3,2:T(1,128)S(1)}, u32[]{:S(2)}, u32[]{:S(2)}) collective-permute-start(f32[1,128,1,32]{1,0,3,2:T(1,128)S(1)} %slice.103), channel_id=1, source_target_pairs={{1,0},{2,1},{3,2},{4,3},{5,4},{6,5},{7,6},{9,8},{10,9},{11,10},{12... | collective-permute-start | bytes 49160 | tf_op jit(solution)/shard_map/ppermute | solution.py:11
  88.5 8.4 %copy-start.4 = (f32[8,1,64,64]{3,0,2,1:T(8,128)S(1)}, f32[8,1,64,64]{3,0,2,1:T(8,128)}, u32[]{:S(2)}) copy-start(f32[8,1,64,64]{3,0,2,1:T(8,128)} %slice.110) | copy-start | bytes 393220
  88.5 8.4 %copy-start.1 = (bf16[1,160,17,128]{1,0,3,2:T(2,128)(2,1)S(1)}, bf16[1,160,17,128]{1,0,3,2:T(2,128)(2,1)}, u32[]{:S(2)}) copy-start(bf16[1,160,17,128]{1,0,3,2:T(2,128)(2,1)} %pad_maximum_fusion) | copy-start | bytes 2088964
  88.5 8.3 %collective-permute-start.6 = (f32[1,64,1,64]{1,3,2,0:T(8,128)S(1)}, f32[1,64,1,64]{1,3,2,0:T(8,128)S(1)}, u32[]{:S(2)}, u32[]{:S(2)}) collective-permute-start(f32[1,64,1,64]{1,3,2,0:T(8,128)S(1)} %slice.109), channel_id=1, source_target_pairs={{1,0},{2,1},{3,2},{4,3},{5,4},{6,5},{7,6},{9,8},{10,9},{11,10},{12... | collective-permute-start | bytes 49160 | tf_op jit(solution)/shard_map/ppermute | solution.py:11
  102.6 550.5 %all-reduce.7.cloned.1.call-start = ((), (), s32[]{:S(2)}) async-start(), calls=%async_computation.1 | async-start | bytes 13860864 | tf_op jit(solution)/shard_map/psum | solution.py:104
  353.2 0.7 copy-start.13
  653.1 3.8 copy-start.2
Sparse Core Ops, SparseCore 0:
  102.7 250.4 all-reduce.4
  356.1 296.9 all-reduce.6
